TPU v7x, 256 devices: a whole 4x4x8 slice. The times are simulated.
256 devices in a mesh: rows: 256 (over x, z, y, core).
Axes of the slice: x: 4, y: 4, z: 8, core: 2. Of those that a mesh axis runs over, the one named last changes fastest.
Arguments:
- residual: float32 [131072, 128], P('rows'), may hold values from -6 to 6
- inv_diag: float32 [131072, 512], P('rows'), may hold values from -0.25 to 0.25
- coupling_tiles: float32 [131072, 6, 512], P('rows'), may hold values from -0.0546875 to 0.0546875
- colour: int32 [256], P('rows'), may hold values from 0 to 3, as said below
- tile_cols: int32 [256, 6], P('rows'), may hold values from 0 to 255, as said below
Outputs:
- precond: float32 [131072, 128], P('rows')
Inputs may be any that keep to these rules, and one draw needn't show every extreme that they name: Every aligned group of 4 blocks (blocks 4 g to 4 g + 3) holds each colour exactly once. `tile_cols`: row b lists 6 distinct blocks, each within 4 places of b along the cycle of blocks (indices modulo 256), none equal to b and none of b's colour.
All inputs are finite; a program needn't handle non-finite values.
Results may differ from a plain program's by a relative error of at most 0.0001.
Values sent between devices are 32-bit elements; how exact they have to be, the bound alone decides.
A program may use at most 128 MiB of HBM per device.

v0:
```python
import jax
import jax.numpy as jnp
from jax import lax
from jax.sharding import PartitionSpec as P

BLOCK = 512
COLS = 128
TILES = 6
COLOURS = 4
REACH = 4


def from_behind(value, axis, by):
    count = lax.axis_size(axis)
    return lax.ppermute(value, axis, [(i, (i + by) % count) for i in range(count)])


def neighbour_blocks(current):
    from_below = []
    from_above = []
    for distance in range(1, REACH + 1):
        from_below.append(from_behind(current, "rows", distance))
        from_above.append(from_behind(current, "rows", -distance))
    return jnp.stack(from_below[::-1] + from_above)


def per_device(residual, inv_diag, coupling_tiles, colour, tile_cols):
    cycle_size = lax.axis_size("rows")
    myself = lax.axis_index("rows")
    own_colour = colour[0]
    relative = (tile_cols[0] - myself) % cycle_size
    signed = jnp.where(relative > cycle_size // 2, relative - cycle_size, relative)
    offset_table = jnp.concatenate([jnp.arange(-REACH, 0), jnp.arange(1, REACH + 1)])
    selector = (signed[:, None] == offset_table[None, :]).astype(jnp.float32)
    flat_tiles = coupling_tiles.reshape(BLOCK, TILES * BLOCK)

    def relax_block(current, near_cache, colour_now):

        def solve_block(operand):
            picked = jnp.einsum(
                "ko,orc->krc", selector, near_cache, precision=lax.Precision.HIGHEST
            )
            picked = picked.reshape(TILES * BLOCK, COLS)
            coupled = jnp.dot(flat_tiles, picked, precision=lax.Precision.HIGHEST)
            return jnp.dot(inv_diag, residual - coupled, precision=lax.Precision.HIGHEST)

        return lax.cond(own_colour == colour_now, solve_block, lambda operand: operand, current)

    current = jnp.zeros(residual.shape, jnp.float32)
    near_cache = jnp.zeros((2 * REACH,) + residual.shape, jnp.float32)
    for colour_now in range(COLOURS):
        current = relax_block(current, near_cache, colour_now)
        near_cache = neighbour_blocks(current)
    for colour_now in range(COLOURS - 1, 0, -1):
        current = relax_block(current, near_cache, colour_now)
        near_cache = neighbour_blocks(current)
    return relax_block(current, near_cache, 0)


def solution(mesh):
    in_specs = (P("rows", None), P("rows", None), P("rows", None, None), P("rows"), P("rows", None))
    out_specs = P("rows", None)
    return jax.shard_map(
        per_device, mesh=mesh, in_specs=in_specs, out_specs=out_specs, check_vma=False
    )
```

profile of v0, /device:TPU:9, one launch (start us, length us, event | category | flops | bytes accessed | tf_op | source)
XLA Modules:
  0.0 438.9 jit_solution(16274030301416175959)
XLA Ops:
  0.7 6.6 %copy.74 = f32[512,6,512]{0,2,1:T(8,128)} copy(f32[512,6,512]{2,0,1:T(8,128)} %param.23) | data formatting | bytes 12582912 | tf_op args[2]
  7.5 15.4 %conditional.8 = (f32[512,128]{0,1:T(8,128)S(1)}) conditional(s32[]{:T(128)} %bitcast.33, () %tuple.53, (f32[6,8]{1,0:T(8,128)S(1)}, f32[512,3072]{0,1:T(8,128)}, f32[512,128]{1,0:T(8,128)S(1)}, f32[512,512]{1,0:T(8,128)S(1)}) %tuple.106), branch_computations={%region_0.1_spmd, %region_1.2_spmd} | conditional | flops 2856386560 | bytes 14680264 | solution.py:47
  9.6 12.0 %fusion = f32[512,128]{1,0:T(8,128)S(1)} fusion(f32[512,128]{1,0:T(8,128)S(1)} %get-tuple-element.114, f32[3072,128]{1,0:T(8,128)S(1)} %bitcast.192, f32[512,3072]{0,1:T(8,128)} %get-tuple-element.155), kind=kOutput, calls=%fused_computation.3 | convolution fusion | flops 2415984640 | bytes 8388608 | tf_op jit(solution)/shard_map/cond/branch_1_fun/dot_general | solution.py:44
  23.8 12.2 %collective-permute-start.5 = (f32[512,128]{1,0:T(8,128)}, f32[512,128]{1,0:T(8,128)S(1)}, u32[]{:S(2)}, u32[]{:S(2)}) collective-permute-start(f32[512,128]{1,0:T(8,128)} %copy.76), channel_id=1, source_target_pairs={{0,254},{1,255},{2,0},{3,1},{4,2},{5,3},{6,4},{7,5},{8,6},{9,7},{1... | collective-permute-start | bytes 786440 | tf_op jit(solution)/shard_map/ppermute | solution.py:15
  35.9 12.5 %collective-permute-start.3 = (f32[512,128]{1,0:T(8,128)}, f32[512,128]{1,0:T(8,128)S(1)}, u32[]{:S(2)}, u32[]{:S(2)}) collective-permute-start(f32[512,128]{1,0:T(8,128)} %copy.76), channel_id=1, source_target_pairs={{0,1},{1,2},{2,3},{3,4},{4,5},{5,6},{6,7},{7,8},{8,9},{9,10},{10,1... | collective-permute-start | bytes 786440 | tf_op jit(solution)/shard_map/ppermute | solution.py:15
  61.6 17.7 %collective-permute-done = f32[512,128]{1,0:T(8,128)} collective-permute-done((f32[512,128]{1,0:T(8,128)}, f32[512,128]{1,0:T(8,128)}, u32[]{:S(2)}, u32[]{:S(2)}) %collective-permute-start) | collective-permute-done | bytes 262176 | tf_op jit(solution)/shard_map/ppermute | solution.py:15
  86.3 8.4 %collective-permute-start.13 = (f32[512,128]{1,0:T(8,128)}, f32[512,128]{1,0:T(8,128)S(1)}, u32[]{:S(2)}, u32[]{:S(2)}) collective-permute-start(f32[512,128]{1,0:T(8,128)} %copy.85), channel_id=1, source_target_pairs={{0,254},{1,255},{2,0},{3,1},{4,2},{5,3},{6,4},{7,5},{8,6},{9,7},{1... | collective-permute-start | bytes 786440 | tf_op jit(solution)/shard_map/ppermute | solution.py:15
  94.7 10.0 %collective-permute-start.12 = (f32[512,128]{1,0:T(8,128)}, f32[512,128]{1,0:T(8,128)S(1)}, u32[]{:S(2)}, u32[]{:S(2)}) collective-permute-start(f32[512,128]{1,0:T(8,128)} %copy.85), channel_id=1, source_target_pairs={{0,255},{1,0},{2,1},{3,2},{4,3},{5,4},{6,5},{7,6},{8,7},{9,8},{10,... | collective-permute-start | bytes 786440 | tf_op jit(solution)/shard_map/ppermute | solution.py:15
  112.7 7.3 %collective-permute-start.9 = (f32[512,128]{1,0:T(8,128)}, f32[512,128]{1,0:T(8,128)S(1)}, u32[]{:S(2)}, u32[]{:S(2)}) collective-permute-start(f32[512,128]{1,0:T(8,128)} %copy.85), channel_id=1, source_target_pairs={{0,3},{1,4},{2,5},{3,6},{4,7},{5,8},{6,9},{7,10},{8,11},{9,12},{10... | collective-permute-start | bytes 786440 | tf_op jit(solution)/shard_map/ppermute | solution.py:15
  145.2 10.3 %collective-permute-start.22 = (f32[512,128]{1,0:T(8,128)}, f32[512,128]{1,0:T(8,128)S(1)}, u32[]{:S(2)}, u32[]{:S(2)}) collective-permute-start(f32[512,128]{1,0:T(8,128)} %copy.94), channel_id=1, source_target_pairs={{0,253},{1,254},{2,255},{3,0},{4,1},{5,2},{6,3},{7,4},{8,5},{9,6},... | collective-permute-start | bytes 786440 | tf_op jit(solution)/shard_map/ppermute | solution.py:15
  163.2 7.6 %collective-permute-start.17 = (f32[512,128]{1,0:T(8,128)}, f32[512,128]{1,0:T(8,128)S(1)}, u32[]{:S(2)}, u32[]{:S(2)}) collective-permute-start(f32[512,128]{1,0:T(8,128)} %copy.94), channel_id=1, source_target_pairs={{0,3},{1,4},{2,5},{3,6},{4,7},{5,8},{6,9},{7,10},{8,11},{9,12},{10... | collective-permute-start | bytes 786440 | tf_op jit(solution)/shard_map/ppermute | solution.py:15
  177.0 10.9 %collective-permute-done.16 = f32[512,128]{1,0:T(8,128)} collective-permute-done((f32[512,128]{1,0:T(8,128)}, f32[512,128]{1,0:T(8,128)}, u32[]{:S(2)}, u32[]{:S(2)}) %collective-permute-start.16) | collective-permute-done | bytes 262176 | tf_op jit(solution)/shard_map/ppermute | solution.py:15
  199.9 13.8 %collective-permute-start.31 = (f32[512,128]{1,0:T(8,128)}, f32[512,128]{1,0:T(8,128)S(1)}, u32[]{:S(2)}, u32[]{:S(2)}) collective-permute-start(f32[512,128]{1,0:T(8,128)} %copy.103), channel_id=1, source_target_pairs={{0,252},{1,253},{2,254},{3,255},{4,0},{5,1},{6,2},{7,3},{8,4},{9,5... | collective-permute-start | bytes 786440 | tf_op jit(solution)/shard_map/ppermute | solution.py:15
  232.9 14.2 %collective-permute-done.24 = f32[512,128]{1,0:T(8,128)} collective-permute-done((f32[512,128]{1,0:T(8,128)}, f32[512,128]{1,0:T(8,128)}, u32[]{:S(2)}, u32[]{:S(2)}) %collective-permute-start.24) | collective-permute-done | bytes 262176 | tf_op jit(solution)/shard_map/ppermute | solution.py:15
  258.9 10.0 %collective-permute-start.39 = (f32[512,128]{1,0:T(8,128)}, f32[512,128]{1,0:T(8,128)S(1)}, u32[]{:S(2)}, u32[]{:S(2)}) collective-permute-start(f32[512,128]{1,0:T(8,128)} %copy.112), channel_id=1, source_target_pairs={{0,252},{1,253},{2,254},{3,255},{4,0},{5,1},{6,2},{7,3},{8,4},{9,5... | collective-permute-start | bytes 786440 | tf_op jit(solution)/shard_map/ppermute | solution.py:15
  289.8 15.8 %collective-permute-done.32 = f32[512,128]{1,0:T(8,128)} collective-permute-done((f32[512,128]{1,0:T(8,128)}, f32[512,128]{1,0:T(8,128)}, u32[]{:S(2)}, u32[]{:S(2)}) %collective-permute-start.32) | collective-permute-done | bytes 262176 | tf_op jit(solution)/shard_map/ppermute | solution.py:15
  318.2 10.1 %collective-permute-start.46 = (f32[512,128]{1,0:T(8,128)}, f32[512,128]{1,0:T(8,128)S(1)}, u32[]{:S(2)}, u32[]{:S(2)}) collective-permute-start(f32[512,128]{1,0:T(8,128)} %copy.121), channel_id=1, source_target_pairs={{0,253},{1,254},{2,255},{3,0},{4,1},{5,2},{6,3},{7,4},{8,5},{9,6},... | collective-permute-start | bytes 786440 | tf_op jit(solution)/shard_map/ppermute | solution.py:15
  334.0 7.1 %collective-permute-done.45 = f32[512,128]{1,0:T(8,128)S(1)} collective-permute-done((f32[512,128]{1,0:T(8,128)}, f32[512,128]{1,0:T(8,128)S(1)}, u32[]{:S(2)}, u32[]{:S(2)}) %collective-permute-start.45) | collective-permute-done | bytes 262176 | tf_op jit(solution)/shard_map/ppermute | solution.py:15
  348.6 14.3 %collective-permute-done.40 = f32[512,128]{1,0:T(8,128)} collective-permute-done((f32[512,128]{1,0:T(8,128)}, f32[512,128]{1,0:T(8,128)}, u32[]{:S(2)}, u32[]{:S(2)}) %collective-permute-start.40) | collective-permute-done | bytes 262176 | tf_op jit(solution)/shard_map/ppermute | solution.py:15
  375.3 10.9 %collective-permute-start.53 = (f32[512,128]{1,0:T(8,128)}, f32[512,128]{1,0:T(8,128)S(1)}, u32[]{:S(2)}, u32[]{:S(2)}) collective-permute-start(f32[512,128]{1,0:T(8,128)} %copy.130), channel_id=1, source_target_pairs={{0,254},{1,255},{2,0},{3,1},{4,2},{5,3},{6,4},{7,5},{8,6},{9,7},{1... | collective-permute-start | bytes 786440 | tf_op jit(solution)/shard_map/ppermute | solution.py:15
  389.4 7.4 %collective-permute-done.54 = f32[512,128]{1,0:T(8,128)S(1)} collective-permute-done((f32[512,128]{1,0:T(8,128)}, f32[512,128]{1,0:T(8,128)S(1)}, u32[]{:S(2)}, u32[]{:S(2)}) %collective-permute-start.54) | collective-permute-done | bytes 262176 | tf_op jit(solution)/shard_map/ppermute | solution.py:15
  408.2 8.0 %collective-permute-done.48 = f32[512,128]{1,0:T(8,128)} collective-permute-done((f32[512,128]{1,0:T(8,128)}, f32[512,128]{1,0:T(8,128)}, u32[]{:S(2)}, u32[]{:S(2)}) %collective-permute-start.48) | collective-permute-done | bytes 262176 | tf_op jit(solution)/shard_map/ppermute | solution.py:15
  422.2 15.6 %conditional.15 = (f32[512,128]{0,1:T(8,128)S(1)}) conditional(s32[]{:T(128)} %bitcast.33, f32[512,128]{0,1:T(8,128)S(1)} %get-tuple-element.203, (f32[6,8]{1,0:T(8,128)S(1)}, f32[8,512,128]{2,0,1:T(8,128)}, f32[512,3072]{0,1:T(8,128)}, f32[512,128]{1,0:T(8,128)S(1)}, f32[512,512]{1,0:T(8,128)S(1)}) %tuple.113), branch_computations={%region_14.15_spmd, %region_15.16_spmd} | conditional | flops 2856386560 | bytes 41943268 | solution.py:47
  426.3 10.0 %fusion.22 = f32[512,128]{1,0:T(8,128)S(1)} fusion(f32[512,128]{1,0:T(8,128)S(1)} %get-tuple-element.148, f32[3072,128]{1,0:T(8,128)S(1)} %bitcast.199, f32[512,3072]{0,1:T(8,128)S(1)} %copy-done.6), kind=kOutput, calls=%fused_computation.39 | convolution fusion | flops 2415984640 | bytes 8388608 | tf_op jit(solution)/shard_map/cond/branch_1_fun/dot_general | solution.py:44
  (132 shorter events, 200.2 us)
Async XLA Ops:
  23.8 24.7 %collective-permute-start.7 = (f32[512,128]{1,0:T(8,128)}, f32[512,128]{1,0:T(8,128)S(1)}, u32[]{:S(2)}, u32[]{:S(2)}) collective-permute-start(f32[512,128]{1,0:T(8,128)} %copy.76), channel_id=1, source_target_pairs={{0,252},{1,253},{2,254},{3,255},{4,0},{5,1},{6,2},{7,3},{8,4},{9,5... | collective-permute-start | bytes 786440 | tf_op jit(solution)/shard_map/ppermute | solution.py:15
  23.8 24.7 %collective-permute-start.6 = (f32[512,128]{1,0:T(8,128)}, f32[512,128]{1,0:T(8,128)S(1)}, u32[]{:S(2)}, u32[]{:S(2)}) collective-permute-start(f32[512,128]{1,0:T(8,128)} %copy.76), channel_id=1, source_target_pairs={{0,253},{1,254},{2,255},{3,0},{4,1},{5,2},{6,3},{7,4},{8,5},{9,6},... | collective-permute-start | bytes 786440 | tf_op jit(solution)/shard_map/ppermute | solution.py:15
  23.8 28.0 %collective-permute-start.5 = (f32[512,128]{1,0:T(8,128)}, f32[512,128]{1,0:T(8,128)S(1)}, u32[]{:S(2)}, u32[]{:S(2)}) collective-permute-start(f32[512,128]{1,0:T(8,128)} %copy.76), channel_id=1, source_target_pairs={{0,254},{1,255},{2,0},{3,1},{4,2},{5,3},{6,4},{7,5},{8,6},{9,7},{1... | collective-permute-start | bytes 786440 | tf_op jit(solution)/shard_map/ppermute | solution.py:15
  35.9 18.3 %collective-permute-start.3 = (f32[512,128]{1,0:T(8,128)}, f32[512,128]{1,0:T(8,128)S(1)}, u32[]{:S(2)}, u32[]{:S(2)}) collective-permute-start(f32[512,128]{1,0:T(8,128)} %copy.76), channel_id=1, source_target_pairs={{0,1},{1,2},{2,3},{3,4},{4,5},{5,6},{6,7},{7,8},{8,9},{9,10},{10,1... | collective-permute-start | bytes 786440 | tf_op jit(solution)/shard_map/ppermute | solution.py:15
  51.8 27.5 %collective-permute-start = (f32[512,128]{1,0:T(8,128)}, f32[512,128]{1,0:T(8,128)}, u32[]{:S(2)}, u32[]{:S(2)}) collective-permute-start(f32[512,128]{1,0:T(8,128)} %copy.76), channel_id=1, source_target_pairs={{0,4},{1,5},{2,6},{3,7},{4,8},{5,9},{6,10},{7,11},{8,12},{9,13},{1... | collective-permute-start | bytes 786440 | tf_op jit(solution)/shard_map/ppermute | solution.py:15
  86.3 20.0 %collective-permute-start.15 = (f32[512,128]{1,0:T(8,128)}, f32[512,128]{1,0:T(8,128)S(1)}, u32[]{:S(2)}, u32[]{:S(2)}) collective-permute-start(f32[512,128]{1,0:T(8,128)} %copy.85), channel_id=1, source_target_pairs={{0,252},{1,253},{2,254},{3,255},{4,0},{5,1},{6,2},{7,3},{8,4},{9,5... | collective-permute-start | bytes 786440 | tf_op jit(solution)/shard_map/ppermute | solution.py:15
  86.3 26.4 %collective-permute-start.14 = (f32[512,128]{1,0:T(8,128)}, f32[512,128]{1,0:T(8,128)S(1)}, u32[]{:S(2)}, u32[]{:S(2)}) collective-permute-start(f32[512,128]{1,0:T(8,128)} %copy.85), channel_id=1, source_target_pairs={{0,253},{1,254},{2,255},{3,0},{4,1},{5,2},{6,3},{7,4},{8,5},{9,6},... | collective-permute-start | bytes 786440 | tf_op jit(solution)/shard_map/ppermute | solution.py:15
  86.3 33.7 %collective-permute-start.13 = (f32[512,128]{1,0:T(8,128)}, f32[512,128]{1,0:T(8,128)S(1)}, u32[]{:S(2)}, u32[]{:S(2)}) collective-permute-start(f32[512,128]{1,0:T(8,128)} %copy.85), channel_id=1, source_target_pairs={{0,254},{1,255},{2,0},{3,1},{4,2},{5,3},{6,4},{7,5},{8,6},{9,7},{1... | collective-permute-start | bytes 786440 | tf_op jit(solution)/shard_map/ppermute | solution.py:15
  94.7 31.7 %collective-permute-start.12 = (f32[512,128]{1,0:T(8,128)}, f32[512,128]{1,0:T(8,128)S(1)}, u32[]{:S(2)}, u32[]{:S(2)}) collective-permute-start(f32[512,128]{1,0:T(8,128)} %copy.85), channel_id=1, source_target_pairs={{0,255},{1,0},{2,1},{3,2},{4,3},{5,4},{6,5},{7,6},{8,7},{9,8},{10,... | collective-permute-start | bytes 786440 | tf_op jit(solution)/shard_map/ppermute | solution.py:15
  104.7 21.8 %collective-permute-start.11 = (f32[512,128]{1,0:T(8,128)}, f32[512,128]{1,0:T(8,128)S(1)}, u32[]{:S(2)}, u32[]{:S(2)}) collective-permute-start(f32[512,128]{1,0:T(8,128)} %copy.85), channel_id=1, source_target_pairs={{0,1},{1,2},{2,3},{3,4},{4,5},{5,6},{6,7},{7,8},{8,9},{9,10},{10,1... | collective-permute-start | bytes 786440 | tf_op jit(solution)/shard_map/ppermute | solution.py:15
  106.3 20.1 %collective-permute-start.10 = (f32[512,128]{1,0:T(8,128)}, f32[512,128]{1,0:T(8,128)S(1)}, u32[]{:S(2)}, u32[]{:S(2)}) collective-permute-start(f32[512,128]{1,0:T(8,128)} %copy.85), channel_id=1, source_target_pairs={{0,2},{1,3},{2,4},{3,5},{4,6},{5,7},{6,8},{7,9},{8,10},{9,11},{10,... | collective-permute-start | bytes 786440 | tf_op jit(solution)/shard_map/ppermute | solution.py:15
  145.2 18.0 %collective-permute-start.22 = (f32[512,128]{1,0:T(8,128)}, f32[512,128]{1,0:T(8,128)S(1)}, u32[]{:S(2)}, u32[]{:S(2)}) collective-permute-start(f32[512,128]{1,0:T(8,128)} %copy.94), channel_id=1, source_target_pairs={{0,253},{1,254},{2,255},{3,0},{4,1},{5,2},{6,3},{7,4},{8,5},{9,6},... | collective-permute-start | bytes 786440 | tf_op jit(solution)/shard_map/ppermute | solution.py:15
  156.1 20.6 %collective-permute-start.20 = (f32[512,128]{1,0:T(8,128)}, f32[512,128]{1,0:T(8,128)S(1)}, u32[]{:S(2)}, u32[]{:S(2)}) collective-permute-start(f32[512,128]{1,0:T(8,128)} %copy.94), channel_id=1, source_target_pairs={{0,255},{1,0},{2,1},{3,2},{4,3},{5,4},{6,5},{7,6},{8,7},{9,8},{10,... | collective-permute-start | bytes 786440 | tf_op jit(solution)/shard_map/ppermute | solution.py:15
  159.0 17.7 %collective-permute-start.19 = (f32[512,128]{1,0:T(8,128)}, f32[512,128]{1,0:T(8,128)S(1)}, u32[]{:S(2)}, u32[]{:S(2)}) collective-permute-start(f32[512,128]{1,0:T(8,128)} %copy.94), channel_id=1, source_target_pairs={{0,1},{1,2},{2,3},{3,4},{4,5},{5,6},{6,7},{7,8},{8,9},{9,10},{10,1... | collective-permute-start | bytes 786440 | tf_op jit(solution)/shard_map/ppermute | solution.py:15
  199.9 19.7 %collective-permute-start.31 = (f32[512,128]{1,0:T(8,128)}, f32[512,128]{1,0:T(8,128)S(1)}, u32[]{:S(2)}, u32[]{:S(2)}) collective-permute-start(f32[512,128]{1,0:T(8,128)} %copy.103), channel_id=1, source_target_pairs={{0,252},{1,253},{2,254},{3,255},{4,0},{5,1},{6,2},{7,3},{8,4},{9,5... | collective-permute-start | bytes 786440 | tf_op jit(solution)/shard_map/ppermute | solution.py:15
  228.4 18.7 %collective-permute-start.24 = (f32[512,128]{1,0:T(8,128)}, f32[512,128]{1,0:T(8,128)}, u32[]{:S(2)}, u32[]{:S(2)}) collective-permute-start(f32[512,128]{1,0:T(8,128)} %copy.103), channel_id=1, source_target_pairs={{0,4},{1,5},{2,6},{3,7},{4,8},{5,9},{6,10},{7,11},{8,12},{9,13},{1... | collective-permute-start | bytes 786440 | tf_op jit(solution)/shard_map/ppermute | solution.py:15
  269.0 16.8 %collective-permute-start.37 = (f32[512,128]{1,0:T(8,128)}, f32[512,128]{1,0:T(8,128)S(1)}, u32[]{:S(2)}, u32[]{:S(2)}) collective-permute-start(f32[512,128]{1,0:T(8,128)} %copy.112), channel_id=1, source_target_pairs={{0,254},{1,255},{2,0},{3,1},{4,2},{5,3},{6,4},{7,5},{8,6},{9,7},{1... | collective-permute-start | bytes 786440 | tf_op jit(solution)/shard_map/ppermute | solution.py:15
  269.0 18.1 %collective-permute-start.36 = (f32[512,128]{1,0:T(8,128)}, f32[512,128]{1,0:T(8,128)S(1)}, u32[]{:S(2)}, u32[]{:S(2)}) collective-permute-start(f32[512,128]{1,0:T(8,128)} %copy.112), channel_id=1, source_target_pairs={{0,255},{1,0},{2,1},{3,2},{4,3},{5,4},{6,5},{7,6},{8,7},{9,8},{10,... | collective-permute-start | bytes 786440 | tf_op jit(solution)/shard_map/ppermute | solution.py:15
  269.7 17.4 %collective-permute-start.35 = (f32[512,128]{1,0:T(8,128)}, f32[512,128]{1,0:T(8,128)S(1)}, u32[]{:S(2)}, u32[]{:S(2)}) collective-permute-start(f32[512,128]{1,0:T(8,128)} %copy.112), channel_id=1, source_target_pairs={{0,1},{1,2},{2,3},{3,4},{4,5},{5,6},{6,7},{7,8},{8,9},{9,10},{10,1... | collective-permute-start | bytes 786440 | tf_op jit(solution)/shard_map/ppermute | solution.py:15
  285.8 19.8 %collective-permute-start.32 = (f32[512,128]{1,0:T(8,128)}, f32[512,128]{1,0:T(8,128)}, u32[]{:S(2)}, u32[]{:S(2)}) collective-permute-start(f32[512,128]{1,0:T(8,128)} %copy.112), channel_id=1, source_target_pairs={{0,4},{1,5},{2,6},{3,7},{4,8},{5,9},{6,10},{7,11},{8,12},{9,13},{1... | collective-permute-start | bytes 786440 | tf_op jit(solution)/shard_map/ppermute | solution.py:15
  341.1 21.8 %collective-permute-start.40 = (f32[512,128]{1,0:T(8,128)}, f32[512,128]{1,0:T(8,128)}, u32[]{:S(2)}, u32[]{:S(2)}) collective-permute-start(f32[512,128]{1,0:T(8,128)} %copy.121), channel_id=1, source_target_pairs={{0,4},{1,5},{2,6},{3,7},{4,8},{5,9},{6,10},{7,11},{8,12},{9,13},{1... | collective-permute-start | bytes 786440 | tf_op jit(solution)/shard_map/ppermute | solution.py:15
  375.0 21.8 %collective-permute-start.54 = (f32[512,128]{1,0:T(8,128)}, f32[512,128]{1,0:T(8,128)S(1)}, u32[]{:S(2)}, u32[]{:S(2)}) collective-permute-start(f32[512,128]{1,0:T(8,128)} %copy.130), channel_id=1, source_target_pairs={{0,253},{1,254},{2,255},{3,0},{4,1},{5,2},{6,3},{7,4},{8,5},{9,6},... | collective-permute-start | bytes 786440 | tf_op jit(solution)/shard_map/ppermute | solution.py:15
  375.3 26.2 %collective-permute-start.53 = (f32[512,128]{1,0:T(8,128)}, f32[512,128]{1,0:T(8,128)S(1)}, u32[]{:S(2)}, u32[]{:S(2)}) collective-permute-start(f32[512,128]{1,0:T(8,128)} %copy.130), channel_id=1, source_target_pairs={{0,254},{1,255},{2,0},{3,1},{4,2},{5,3},{6,4},{7,5},{8,6},{9,7},{1... | collective-permute-start | bytes 786440 | tf_op jit(solution)/shard_map/ppermute | solution.py:15
  386.2 17.9 %collective-permute-start.52 = (f32[512,128]{1,0:T(8,128)}, f32[512,128]{1,0:T(8,128)S(1)}, u32[]{:S(2)}, u32[]{:S(2)}) collective-permute-start(f32[512,128]{1,0:T(8,128)} %copy.130), channel_id=1, source_target_pairs={{0,255},{1,0},{2,1},{3,2},{4,3},{5,4},{6,5},{7,6},{8,7},{9,8},{10,... | collective-permute-start | bytes 786440 | tf_op jit(solution)/shard_map/ppermute | solution.py:15
  (36 other events, 462.4 us)
where the time goes:
time: 444 us; the launch traced here: 439 us
  waiting for transfers between devices  169 us (38%)
  starting transfers between devices  156 us (35%)
  local copies, waits for them, and re-layouts  55.8 us (13%)
  matrix products  29.9 us (7%)
  loops' own time  26.6 us (6%)
    ppermute x56, waiting for transfers between devices, from_behind(): lax.ppermute(value, axis, [(i, (i + by) % count) for i in range(count)])  169 us
    ppermute x56, starting transfers between devices, from_behind(): lax.ppermute(value, axis, [(i, (i + by) % count) for i in range(count)])  156 us
    another operation x7, local copies, waits for them, and re-layouts, neighbour_blocks(): return jnp.stack(from_below[::-1] + from_above)  41.8 us
    another operation x8, loops' own time, relax_block(): lax.cond(own_colour == colour_now, solve_block, lambda operand: operand,...  26.6 us
    dot_general x2, matrix products, solve_block(): coupled = jnp.dot(flat_tiles, picked, precision=lax.Precision.HIGHEST)  22.1 us
  transfers between devices with their start and end apart: 56, of which 30 were waited for; matrix products, arithmetic and copies ran while one was open for 0% of the time, Pallas kernels for 0%

commit v1 on v0

v1 whole, which is shorter than its diff:
```python
import functools

import jax
import jax.numpy as jnp
from jax import lax
from jax.experimental import pallas as pl
from jax.experimental.pallas import tpu as pltpu
from jax.sharding import PartitionSpec as P

BLOCK = 512
HALF = BLOCK // 2
COLS = 128
TILES = 6
COLOURS = 4
EXCHANGES = 6
WINDOW = 12
CHAINS = 2
NSUB = 1
PIECE = HALF // CHAINS
SUB = PIECE // NSUB
HOPS = (2, -2, 1, -1)
MESH = pl.DeviceIdType.MESH
BF = jnp.bfloat16
F32 = jnp.float32

DUP = len(HOPS)
KINDS = DUP + 5


def split(v):
    hi = v.astype(BF)
    return hi, (v - hi.astype(F32)).astype(BF)


def mm(a, b):
    return jnp.dot(a, b, preferred_element_type=F32)


def swap(v):
    return pltpu.roll(v, COLS // 2, 1)


def left_lanes(rows):
    return lax.broadcasted_iota(jnp.int32, (rows, COLS), 1) < COLS // 2


def kernel(n, colour_ref, tc_ref, res_hbm, inv_hbm, coup_hbm, out_ref,
           res, inv, coup, dsplit, wf, wland, wst, rhs, xin, y, ysend, contrib, tmp, keep_x,
           info, info_smem, tab,
           load_sem, info_send, info_recv, w_send, w_recv, y_sem, x_send, x_recv, smem_sem):
    me = lax.axis_index("rows")
    core = lax.rem(me, 2)
    partner = me + 1 - 2 * core
    pos = lax.rem(me, 4)
    q = lax.rem(me // 2, 2)
    first = me - pos + n - 4
    left = left_lanes(PIECE)

    loads = [
        pltpu.make_async_copy(inv_hbm, inv, load_sem.at[0]),
        pltpu.make_async_copy(res_hbm, res, load_sem.at[1]),
    ]
    for cp in loads:
        cp.start()

    def tile_load(k):
        return pltpu.make_async_copy(coup_hbm.at[k], coup.at[k], load_sem.at[2 + k])

    for k in range(TILES):
        tile_load(k).start()

    others = [4 + lax.rem(pos + r, 4) for r in range(1, 4)] + [0, 1, 2, 3, 8, 9, 10, 11]
    barrier = pltpu.get_barrier_semaphore()
    for t in others:
        pl.semaphore_signal(barrier, inc=1, device_id=(lax.rem(first + t, n),), device_id_type=MESH)

    lane = lax.broadcasted_iota(jnp.int32, (8, 128), 1)
    packed = jnp.where(lane == 0, colour_ref[0], 0)
    for k in range(TILES):
        packed = jnp.where(lane == k + 1, tc_ref[0, k], packed)
    info[4 + pos] = packed

    def pack(v):
        top, bottom = v[0:PIECE], v[PIECE:]
        return jnp.where(left, top, swap(bottom)), jnp.where(left, swap(top), bottom)

    for cp in loads:
        cp.wait()
    dh, dl = split(inv[...])
    dsplit[0:BLOCK] = dh
    dsplit[BLOCK:] = dl
    rh, rl = split(res[...])
    prod = mm(dsplit[...], jnp.concatenate([rh, rl], axis=1))
    prod = prod[0:BLOCK] + prod[BLOCK:]
    prod = prod[:, 0:COLS] + prod[:, COLS:]
    for half in range(2):
        pieces = pack(prod[half * HALF:(half + 1) * HALF])
        for h in range(CHAINS):
            ysend[half, h] = pieces[h]
    y[core] = ysend[core]

    pl.semaphore_wait(barrier, len(others))

    y_copy = pltpu.make_async_remote_copy(
        src_ref=ysend.at[1 - core], dst_ref=y.at[core], send_sem=y_sem.at[0], recv_sem=y_sem.at[1],
        device_id=(partner,), device_id_type=MESH)
    y_copy.start()

    def info_copy(t, slot):
        return pltpu.make_async_remote_copy(
            src_ref=info.at[4 + pos], dst_ref=info.at[slot],
            send_sem=info_send.at[t], recv_sem=info_recv.at[slot],
            device_id=(lax.rem(first + t, n),), device_id_type=MESH)

    def slot_there(t):
        group = t // 4 if isinstance(t, int) else 1
        return 4 * (2 - group) + pos

    for t in others:
        info_copy(t, slot_there(t)).start()

    own_colour = colour_ref[0]

    def active(c):
        return jnp.where(own_colour == c, core, 1 - core)

    def piece(h, par, off, half, j):
        return xin.at[h, par, off, half, pl.ds(j * SUB, SUB)]

    def out_copy(h, par, i, j):
        return pltpu.make_async_remote_copy(
            src_ref=piece(h, par, 2, core, j), dst_ref=piece(h, par, 2 - HOPS[i], core, j),
            send_sem=x_send.at[h, par, i, j], recv_sem=x_recv.at[h, par, i, j],
            device_id=(lax.rem(me + 2 * HOPS[i] + n, n),), device_id_type=MESH)

    def dup(h, par, off, j):
        return pltpu.make_async_remote_copy(
            src_ref=piece(h, par, off, core, j), dst_ref=piece(h, par, off, core, j),
            send_sem=x_send.at[h, par, DUP + off, j], recv_sem=x_recv.at[h, par, DUP + off, j],
            device_id=(partner,), device_id_type=MESH)

    def dup_wait(h, par, off, j):
        pltpu.make_async_remote_copy(
            src_ref=piece(h, par, off, 1 - core, j), dst_ref=piece(h, par, off, 1 - core, j),
            send_sem=x_send.at[h, par, DUP + off, j], recv_sem=x_recv.at[h, par, DUP + off, j],
            device_id=(partner,), device_id_type=MESH).wait_recv()

    def send(h, par):
        for j in range(NSUB):
            for i in range(len(HOPS)):
                out_copy(h, par, i, j).start()
        for j in range(NSUB):
            dup(h, par, 2, j).start()

    y_copy.wait()
    for h in range(CHAINS):
        xin[h, 0, 2, core] = y[active(0), h]
        send(h, 0)

    for c in range(COLOURS):
        for a in range(2):
            for h in range(CHAINS):
                contrib[h, a, c] = jnp.zeros((PIECE, COLS), F32)
    wst[6] = jnp.zeros((BLOCK, BLOCK), BF)
    wst[13] = jnp.zeros((BLOCK, BLOCK), BF)

    def w_copy(k):
        return pltpu.make_async_remote_copy(
            src_ref=wf.at[k, 1 - core], dst_ref=wland.at[k], send_sem=w_send.at[k], recv_sem=w_recv.at[k],
            device_id=(partner,), device_id_type=MESH)

    def premultiply(k, carry):
        tile_load(k).wait()
        ah, al = split(coup[k])
        high = mm(dsplit[...], ah)
        w = high[0:BLOCK] + high[BLOCK:] + mm(dsplit[0:BLOCK], al)
        wf[k, 0] = w[0:HALF]
        wf[k, 1] = w[HALF:]
        w_copy(k).start()
        hi, lo = split(wf[k, core])
        wst[core * 7 + k, 0:HALF] = hi
        wst[core * 7 + k, HALF:] = lo
        return carry

    lax.fori_loop(0, TILES, premultiply, 0)

    for t in others:
        info_copy(t, t).wait_recv()
        info_copy(t, slot_there(t)).wait_send()
    to_smem = pltpu.make_async_copy(info, info_smem, smem_sem)
    to_smem.start()
    to_smem.wait()
    for c in range(COLOURS):
        for sl in range(3):
            where = jnp.int32(0)
            for t in range(1, 4):
                where = jnp.where(info_smem[4 * sl + t, 0, 0] == c, t, where)
            owner = first + 4 * sl + where
            owner = jnp.where(owner >= 2 * n, owner - 2 * n, jnp.where(owner >= n, owner - n, owner))
            off = 2 * (sl - 1) + jnp.where(where >= 2, 1, 0) - q + 2
            off = jnp.where(off < 0, 2, jnp.where(off > 4, 2, off))
            tab[c * 9 + sl] = off
            for a in range(2):
                index = jnp.int32(6)
                slot = 4 + 2 * q + a
                for k in range(TILES):
                    index = jnp.where(info_smem[slot, 0, k + 1] == owner, k, index)
                tab[c * 9 + 3 + 3 * a + sl] = a * 7 + index

    def receive_w(k, carry):
        w_copy(k).wait()
        hi, lo = split(wland[k])
        wst[(1 - core) * 7 + k, 0:HALF] = hi
        wst[(1 - core) * 7 + k, HALF:] = lo
        return carry

    lax.fori_loop(0, TILES, receive_w, 0)

    def colour_of(s):
        return jnp.where(s <= 3, s, 6 - s)

    def make_rhs(h, par, c, sl):
        near, far = ((1, 0), (2, 3 - 2 * q), (3, 4))[sl]
        v = jnp.where(tab[c * 9 + sl] == near, xin[h, par, near], xin[h, par, far])
        for half in range(2):
            hi = v[half].astype(BF).astype(F32)
            lo = v[half] - hi
            row = half * HALF
            rhs[h, sl, row:row + PIECE] = jnp.where(left, hi, swap(lo)).astype(BF)
            rhs[h, sl, row + PIECE:row + HALF] = jnp.where(left, swap(hi), lo).astype(BF)

    def product(h, c, a, sl):
        return mm(wst[tab[c * 9 + 3 + 3 * a + sl]], rhs[h, sl])

    def fold(v):
        v = v[0:HALF] + v[HALF:]
        v = v + swap(v)
        return jnp.where(left, v[0:PIECE], v[PIECE:])

    def relax(h, s):
        par = lax.rem(s, 2)
        c = colour_of(s)
        nxt = active(colour_of(s + 1))
        for i in reversed(range(len(HOPS))):
            for j in range(NSUB):
                out_copy(h, par, i, j).wait_recv()
                dup(h, par, 2 - HOPS[i], j).start()
        base = y[nxt, h]
        for cc in range(COLOURS):
            base = base - jnp.where(c == cc, 0.0, contrib[h, nxt, cc])
        for off in (2, 1, 3):
            for j in range(NSUB):
                dup_wait(h, par, off, j)
        make_rhs(h, par, c, 1)
        acc = product(h, c, nxt, 1)
        for off in (0, 4):
            for j in range(NSUB):
                dup_wait(h, par, off, j)
        make_rhs(h, par, c, 0)
        make_rhs(h, par, c, 2)
        acc = acc + product(h, c, nxt, 0) + product(h, c, nxt, 2)
        mine = fold(acc)
        xin[h, 1 - par, 2, core] = base - mine
        tmp[...] = mine
        for j in range(NSUB):
            for off in range(5):
                dup(h, par, off, j).wait_send()

        @pl.when(s < EXCHANGES - 1)
        def _():
            send(h, 1 - par)

        keep_x[h] = jnp.where(own_colour == c, xin[h, par, 2], keep_x[h])

        @pl.when(s < EXCHANGES - 1)
        def _():
            other = fold(product(h, c, 1 - nxt, 0) + product(h, c, 1 - nxt, 1) + product(h, c, 1 - nxt, 2))
            mine = tmp[...]
            contrib[h, 0, c] = jnp.where(nxt == 0, mine, other)
            contrib[h, 1, c] = jnp.where(nxt == 0, other, mine)

        for j in range(NSUB):
            for i in range(len(HOPS)):
                out_copy(h, par, i, j).wait_send()

    def stage(s, carry):
        for h in range(CHAINS):
            relax(h, s)
        return carry

    keep_x[...] = jnp.zeros_like(keep_x)
    lax.fori_loop(0, EXCHANGES, stage, 0)

    for h in range(CHAINS):
        for j in range(NSUB):
            dup(h, 0, 2, j).start()
    for h in range(CHAINS):
        for j in range(NSUB):
            dup_wait(h, 0, 2, j)
            dup(h, 0, 2, j).wait_send()
    for half in range(2):
        p0, p1 = (jnp.where(own_colour == 0, xin[h, 0, 2, half], keep_x[h, half]) for h in range(CHAINS))
        out_ref[half * HALF:half * HALF + PIECE] = jnp.where(left, p0, swap(p1))
        out_ref[half * HALF + PIECE:(half + 1) * HALF] = jnp.where(left, swap(p0), p1)


def per_device(n, residual, inv_diag, coupling_tiles, colour, tile_cols):
    tiles = jnp.transpose(coupling_tiles, (1, 0, 2))
    smem = pl.BlockSpec(memory_space=pltpu.SMEM)
    hbm = pl.BlockSpec(memory_space=pl.ANY)
    return pl.pallas_call(
        functools.partial(kernel, n),
        out_shape=jax.ShapeDtypeStruct((BLOCK, COLS), F32),
        in_specs=[smem, smem, hbm, hbm, hbm],
        out_specs=pl.BlockSpec(memory_space=pltpu.VMEM),
        scratch_shapes=[
            pltpu.VMEM((BLOCK, COLS), F32),
            pltpu.VMEM((BLOCK, BLOCK), F32),
            pltpu.VMEM((TILES, BLOCK, BLOCK), F32),
            pltpu.VMEM((2 * BLOCK, BLOCK), BF),
            pltpu.VMEM((TILES, 2, HALF, BLOCK), F32),
            pltpu.VMEM((TILES, HALF, BLOCK), F32),
            pltpu.VMEM((14, BLOCK, BLOCK), BF),
            pltpu.VMEM((CHAINS, 3, BLOCK, COLS), BF),
            pltpu.VMEM((CHAINS, 2, 5, 2, PIECE, COLS), F32),
            pltpu.VMEM((2, CHAINS, PIECE, COLS), F32),
            pltpu.VMEM((2, CHAINS, PIECE, COLS), F32),
            pltpu.VMEM((CHAINS, 2, COLOURS, PIECE, COLS), F32),
            pltpu.VMEM((PIECE, COLS), F32),
            pltpu.VMEM((CHAINS, 2, PIECE, COLS), F32),
            pltpu.VMEM((WINDOW, 8, 128), jnp.int32),
            pltpu.SMEM((WINDOW, 8, 128), jnp.int32),
            pltpu.SMEM((9 * COLOURS,), jnp.int32),
            pltpu.SemaphoreType.DMA((2 + TILES,)),
            pltpu.SemaphoreType.DMA((WINDOW,)),
            pltpu.SemaphoreType.DMA((WINDOW,)),
            pltpu.SemaphoreType.DMA((TILES,)),
            pltpu.SemaphoreType.DMA((TILES,)),
            pltpu.SemaphoreType.DMA((2,)),
            pltpu.SemaphoreType.DMA((CHAINS, 2, KINDS, NSUB)),
            pltpu.SemaphoreType.DMA((CHAINS, 2, KINDS, NSUB)),
            pltpu.SemaphoreType.DMA,
        ],
        compiler_params=pltpu.CompilerParams(
            collective_id=0, has_side_effects=True, vmem_limit_bytes=56 * 1024 * 1024),
    )(colour, tile_cols, residual, inv_diag, tiles)


def solution(mesh):
    in_specs = (P("rows", None), P("rows", None), P("rows", None, None), P("rows"), P("rows", None))
    return jax.shard_map(
        functools.partial(per_device, mesh.shape["rows"]), mesh=mesh, in_specs=in_specs,
        out_specs=P("rows", None), check_vma=False)
```

time: 444 us -> 82.6 us (0.19)
  the two profiles are of different devices: /device:TPU:9 before, /device:TPU:1 now
where the time goes in v1:
time: 82.6 us; the launch traced here: 82.4 us
  Pallas kernels  80.1 us (97%)
  local copies, waits for them, and re-layouts  1.67 us (2%)
    pallas_call x1, Pallas kernels, per_device(): pl.pallas_call(functools.partial(kernel, n), out_shape=jax.ShapeDtypeStru...  80.1 us
    unnamed x1, local copies, waits for them, and re-layouts  1.67 us

profile of v1, /device:TPU:1, one launch (start us, length us, event | category | flops | bytes accessed | tf_op | source)
XLA Modules:
  0.0 82.4 jit_solution(3393852949348524245)
XLA Ops:
  0.7 80.1 %shard_map.55 = f32[512,128]{1,0:T(8,128)} custom-call(s32[1]{0:T(128)S(6)} %copy.7.colour_ref, s32[1,6]{1,0:T(1,128)} %tc_ref.1, f32[512,128]{1,0:T(8,128)} %res_hbm.1, f32[512,512]{1,0:T(8,128)} %inv_hbm.1, f32[6,512,512]{2,1,0:T(8,128)} %bitcast.1), custom_call_target="tpu_custom_call" | custom-call | tf_op jit(solution)/shard_map/pallas_call | solution.py:311
  80.8 1.7 %copy.8 = f32[512,128]{1,0:T(8,128)} copy(f32[512,128]{1,0:T(8,128)} %shard_map.55) | data formatting | bytes 524288

commit v2 on v1

v2 whole, which is shorter than its diff:
```python
import functools

import jax
import jax.numpy as jnp
from jax import lax
from jax.experimental import pallas as pl
from jax.experimental.pallas import tpu as pltpu
from jax.sharding import PartitionSpec as P

BLOCK = 512
COLS = 128
TILES = 6
COLOURS = 4
EXCHANGES = 6
CHAINS = 2
WIDTH = COLS // 2 // CHAINS
GROUPS = COLS // WIDTH
ROWS = BLOCK // GROUPS
HOPS = (2, -2, 1, -1)
MESH = pl.DeviceIdType.MESH
BF = jnp.bfloat16
F32 = jnp.float32


def split(v):
    hi = v.astype(BF)
    return hi, (v - hi.astype(F32)).astype(BF)


def mm(a, b):
    return jnp.dot(a, b, preferred_element_type=F32)


def turn(v, groups):
    shift = groups * WIDTH % COLS
    return pltpu.roll(v, shift, 1) if shift else v


def kernel(n, colour_ref, tc_ref, res_hbm, inv_hbm, coup_hbm, out_ref,
           res, inv, coup, dsplit, wland, wst, rhs, xin, y, ysend, contrib, tmp, acc, keep, fin,
           info, info_smem, tab,
           load_sem, info_send, info_recv, w_send, w_recv, y_sem, x_send, x_recv, fin_sem):
    me = lax.axis_index("rows")
    core = lax.rem(me, 2)
    partner = me + 1 - 2 * core
    q = lax.rem(me // 2, 2)
    upper = lax.rem(me // 4, 2)
    edge = q == upper

    def chip(hop):
        return lax.rem(me + 2 * hop + n, n)

    pos = lax.rem(me, 4)
    first = me - pos + n - 4
    others = [4 + lax.rem(pos + r, 4) for r in range(1, 4)] + [0, 1, 2, 3, 8, 9, 10, 11]
    barrier = pltpu.get_barrier_semaphore()
    for t in others:
        pl.semaphore_signal(barrier, inc=1, device_id=(lax.rem(first + t, n),), device_id_type=MESH)

    loads = [
        pltpu.make_async_copy(inv_hbm, inv, load_sem.at[0]),
        pltpu.make_async_copy(res_hbm, res, load_sem.at[1]),
    ]
    for cp in loads:
        cp.start()

    def tile_load(k):
        return pltpu.make_async_copy(coup_hbm.at[k], coup.at[k], load_sem.at[2 + k])

    for k in range(TILES):
        tile_load(k).start()

    group = lax.broadcasted_iota(jnp.int32, (ROWS, COLS), 1) // WIDTH

    def pick(values):
        v = values[0]
        for g in range(1, GROUPS):
            v = jnp.where(group == g, values[g], v)
        return v

    for cp in loads:
        cp.wait()
    dh, dl = split(inv[...])
    dsplit[0:BLOCK] = dh
    dsplit[BLOCK:] = dl
    rh, rl = split(res[...])
    prod = mm(dsplit[...], jnp.concatenate([rh, rl], axis=1))
    prod = prod[0:BLOCK] + prod[BLOCK:]
    prod = prod[:, 0:COLS] + prod[:, COLS:]
    for j in range(2):
        for h in range(CHAINS):
            ysend[j, h] = pick([turn(prod[r * ROWS:(r + 1) * ROWS], r - j * CHAINS - h) for r in range(GROUPS)])
    y[core] = ysend[core]

    lane = lax.broadcasted_iota(jnp.int32, (8, 128), 1)
    own_colour = colour_ref[0]
    packed = jnp.where(lane == 0, own_colour, me)
    for k in range(TILES):
        packed = jnp.where(lane == k + 1, tc_ref[0, k], packed)
    info[4 + pos] = packed

    pl.semaphore_wait(barrier, len(others))

    y_copy = pltpu.make_async_remote_copy(
        src_ref=ysend.at[1 - core], dst_ref=y.at[core], send_sem=y_sem.at[0], recv_sem=y_sem.at[1],
        device_id=(partner,), device_id_type=MESH)
    y_copy.start()

    def info_copy(t, slot):
        return pltpu.make_async_remote_copy(
            src_ref=info.at[4 + pos], dst_ref=info.at[slot],
            send_sem=info_send.at[t], recv_sem=info_recv.at[slot],
            device_id=(lax.rem(first + t, n),), device_id_type=MESH)

    def slot_there(t):
        group = t // 4 if isinstance(t, int) else 1
        return 4 * (2 - group) + pos

    for t in others:
        info_copy(t, slot_there(t)).start()

    def w_copy(k):
        return pltpu.make_async_remote_copy(
            src_ref=coup.at[k], dst_ref=wland.at[k], send_sem=w_send.at[k], recv_sem=w_recv.at[k],
            device_id=(partner,), device_id_type=MESH)

    def active(c):
        return jnp.where(own_colour == c, core, 1 - core)

    def out_copy(h, par, i):
        return pltpu.make_async_remote_copy(
            src_ref=xin.at[h, par, 2], dst_ref=xin.at[h, par, 2 - HOPS[i]],
            send_sem=x_send.at[h, par, i], recv_sem=x_recv.at[h, par, i],
            device_id=(chip(HOPS[i]),), device_id_type=MESH)

    def send(h, par):
        for i in range(len(HOPS)):
            out_copy(h, par, i).start()

    y_copy.wait()
    for h in range(CHAINS):
        xin[h, 0, 2] = y[active(0), h]
        send(h, 0)
    def premultiply(k, carry):
        tile_load(k).wait()
        ah, al = split(coup[k])
        left = jnp.concatenate([dsplit[0:BLOCK], dsplit[BLOCK:], dsplit[0:BLOCK]], axis=1)
        coup[k] = mm(left, jnp.concatenate([ah, ah, al], axis=0))
        w_copy(k).start()
        hi, lo = split(coup[k])
        wst[core * 7 + k, 0:BLOCK] = hi
        wst[core * 7 + k, BLOCK:] = lo
        return carry

    lax.fori_loop(0, TILES, premultiply, 0)

    for c in range(COLOURS):
        for a in range(2):
            for h in range(CHAINS):
                contrib[h, a, c] = jnp.zeros((ROWS, COLS), F32)
    wst[6] = jnp.zeros((2 * BLOCK, BLOCK), BF)
    wst[13] = jnp.zeros((2 * BLOCK, BLOCK), BF)
    keep[...] = jnp.zeros_like(keep)

    for t in others:
        info_copy(t, t).wait_recv()
        info_copy(t, slot_there(t)).wait_send()
    to_smem = pltpu.make_async_copy(info, info_smem, load_sem.at[0])
    to_smem.start()
    to_smem.wait()
    for c in range(COLOURS):
        for sl in range(3):
            where = jnp.int32(0)
            for t in range(1, 4):
                where = jnp.where(info_smem[4 * sl + t, 0, 0] == c, t, where)
            owner = first + 4 * sl + where
            owner = jnp.where(owner >= 2 * n, owner - 2 * n, jnp.where(owner >= n, owner - n, owner))
            off = 2 * (sl - 1) + jnp.where(where >= 2, 1, 0) - q + 2
            off = jnp.where(off < 0, 2, jnp.where(off > 4, 2, off))
            tab[c * 9 + sl] = off
            for a in range(2):
                index = jnp.int32(6)
                slot = 4 + 2 * q + a
                for k in range(TILES):
                    index = jnp.where(info_smem[slot, 0, k + 1] == owner, k, index)
                tab[c * 9 + 3 + 3 * a + sl] = a * 7 + index
    block_colour = [info_smem[4 + 2 * q + a, 0, 0] for a in range(2)]

    def receive_w(k, carry):
        w_copy(k).wait()
        hi, lo = split(wland[k])
        wst[(1 - core) * 7 + k, 0:BLOCK] = hi
        wst[(1 - core) * 7 + k, BLOCK:] = lo
        return carry

    lax.fori_loop(0, TILES, receive_w, 0)

    def colour_of(s):
        return jnp.where(s <= 3, s, 6 - s)

    def make_rhs(h, par, c, sl):
        near, far = jnp.maximum(2 * sl - q, 0), jnp.minimum(2 * sl - q + 1, 4)
        v = jnp.where(tab[c * 9 + sl] == near, xin[h, par, near], xin[h, par, far])
        hi = v.astype(BF).astype(F32)
        lo = v - hi
        for r in range(GROUPS):
            rows = pl.ds(pl.multiple_of(sl * BLOCK + r * ROWS, ROWS), ROWS)
            rhs[rows, 0:COLS] = jnp.where(group == r, hi, 0.0).astype(BF)
            rhs[rows, COLS:] = jnp.where(group == r, lo, 0.0).astype(BF)

    def product(c, a, slots):
        tiles = [wst[tab[c * 9 + 3 + 3 * a + sl]] for sl in slots]
        ops = [rhs[pl.ds(pl.multiple_of(sl * BLOCK, BLOCK), BLOCK)] for sl in slots]
        return mm(jnp.concatenate(tiles, axis=1), jnp.concatenate(ops, axis=0))

    def fold(v):
        v = v[0:BLOCK] + v[BLOCK:]
        v = v[:, 0:COLS] + v[:, COLS:]
        rows = [v[r * ROWS:(r + 1) * ROWS] for r in range(GROUPS)]
        total = pick(rows)
        for k in range(1, GROUPS):
            total = total + turn(pick([rows[(g - k) % GROUPS] for g in range(GROUPS)]), -k)
        return total

    def relax(h, s):
        par = lax.rem(s, 2)
        c = colour_of(s)
        nxt = active(colour_of(s + 1))
        base = y[nxt, h]
        for cc in range(COLOURS):
            base = base - jnp.where(c == cc, 0.0, contrib[h, nxt, cc])
        early, late = 2 - 2 * upper, 2 * upper

        def arrived(i):
            pltpu.make_async_remote_copy(
                src_ref=xin.at[h, par, 2], dst_ref=xin.at[h, par, 2],
                send_sem=x_send.at[h, par, i], recv_sem=x_recv.at[h, par, i],
                device_id=(partner,), device_id_type=MESH).wait_recv()

        arrived(3 - upper)
        arrived(1 - upper)

        @pl.when(jnp.logical_not(edge))
        def _():
            arrived(2 + upper)

        make_rhs(h, par, c, 1)
        make_rhs(h, par, c, early)
        acc[...] = base - fold(product(c, nxt, (1, early)))

        @pl.when(edge)
        def _():
            arrived(2 + upper)

        arrived(upper)
        make_rhs(h, par, c, late)
        value = acc[...] - fold(product(c, nxt, (late,)))
        xin[h, 1 - par, 2] = value
        tmp[...] = base - value

        @pl.when(s < EXCHANGES - 1)
        def _():
            send(h, 1 - par)

        for a in range(2):
            keep[a, h] = jnp.where(block_colour[a] == c, xin[h, par, 2], keep[a, h])

        @pl.when(s < EXCHANGES - 1)
        def _():
            other = fold(product(c, 1 - nxt, (0, 1, 2)))
            mine = tmp[...]
            contrib[h, 0, c] = jnp.where(nxt == 0, mine, other)
            contrib[h, 1, c] = jnp.where(nxt == 0, other, mine)

        for i in range(len(HOPS)):
            out_copy(h, par, i).wait_send()

    def stage(s, carry):
        for h in range(CHAINS):
            relax(h, s)
        return carry

    lax.fori_loop(0, EXCHANGES, stage, 0)

    for a in range(2):
        for h in range(CHAINS):
            keep[a, h] = jnp.where(block_colour[a] == 0, xin[h, 0, 2], keep[a, h])
    fin[core] = keep[core]
    fin_copy = pltpu.make_async_remote_copy(
        src_ref=keep.at[1 - core], dst_ref=fin.at[core], send_sem=fin_sem.at[0], recv_sem=fin_sem.at[1],
        device_id=(partner,), device_id_type=MESH)
    fin_copy.start()
    fin_copy.wait()
    for r in range(GROUPS):
        out_ref[r * ROWS:(r + 1) * ROWS] = pick(
            [turn(fin[g // CHAINS, g % CHAINS], g - r) for g in range(GROUPS)])


def per_device(n, residual, inv_diag, coupling_tiles, colour, tile_cols):
    tiles = jnp.transpose(coupling_tiles, (1, 0, 2))
    smem = pl.BlockSpec(memory_space=pltpu.SMEM)
    hbm = pl.BlockSpec(memory_space=pl.ANY)
    return pl.pallas_call(
        functools.partial(kernel, n),
        out_shape=jax.ShapeDtypeStruct((BLOCK, COLS), F32),
        in_specs=[smem, smem, hbm, hbm, hbm],
        out_specs=pl.BlockSpec(memory_space=pltpu.VMEM),
        scratch_shapes=[
            pltpu.VMEM((BLOCK, COLS), F32),
            pltpu.VMEM((BLOCK, BLOCK), F32),
            pltpu.VMEM((TILES, BLOCK, BLOCK), F32),
            pltpu.VMEM((2 * BLOCK, BLOCK), BF),
            pltpu.VMEM((TILES, BLOCK, BLOCK), F32),
            pltpu.VMEM((14, 2 * BLOCK, BLOCK), BF),
            pltpu.VMEM((3 * BLOCK, 2 * COLS), BF),
            pltpu.VMEM((CHAINS, 2, 5, ROWS, COLS), F32),
            pltpu.VMEM((2, CHAINS, ROWS, COLS), F32),
            pltpu.VMEM((2, CHAINS, ROWS, COLS), F32),
            pltpu.VMEM((CHAINS, 2, COLOURS, ROWS, COLS), F32),
            pltpu.VMEM((ROWS, COLS), F32),
            pltpu.VMEM((ROWS, COLS), F32),
            pltpu.VMEM((2, CHAINS, ROWS, COLS), F32),
            pltpu.VMEM((2, CHAINS, ROWS, COLS), F32),
            pltpu.VMEM((12, 8, 128), jnp.int32),
            pltpu.SMEM((12, 8, 128), jnp.int32),
            pltpu.SMEM((9 * COLOURS,), jnp.int32),
            pltpu.SemaphoreType.DMA((2 + TILES,)),
            pltpu.SemaphoreType.DMA((12,)),
            pltpu.SemaphoreType.DMA((12,)),
            pltpu.SemaphoreType.DMA((TILES,)),
            pltpu.SemaphoreType.DMA((TILES,)),
            pltpu.SemaphoreType.DMA((2,)),
            pltpu.SemaphoreType.DMA((CHAINS, 2, len(HOPS))),
            pltpu.SemaphoreType.DMA((CHAINS, 2, len(HOPS))),
            pltpu.SemaphoreType.DMA((2,)),
        ],
        compiler_params=pltpu.CompilerParams(
            collective_id=0, has_side_effects=True, vmem_limit_bytes=56 * 1024 * 1024),
    )(colour, tile_cols, residual, inv_diag, tiles)


def solution(mesh):
    in_specs = (P("rows", None), P("rows", None), P("rows", None, None), P("rows"), P("rows", None))
    return jax.shard_map(
        functools.partial(per_device, mesh.shape["rows"]), mesh=mesh, in_specs=in_specs,
        out_specs=P("rows", None), check_vma=False)
```

time: 82.6 us -> 80.9 us (0.979)
  Pallas kernels: 80.1 us -> 78.4 us
    pallas_call x1, Pallas kernels: 80.1 us -> 78.4 us  [per_device(): pl.pallas_call(functools.partial(kernel, n), out_shape=jax.ShapeDtypeStru...]
where the time goes in v2:
time: 80.9 us; the launch traced here: 80.8 us
  Pallas kernels  78.4 us (97%)
  local copies, waits for them, and re-layouts  1.67 us (2%)
    pallas_call x1, Pallas kernels, per_device(): pl.pallas_call(functools.partial(kernel, n), out_shape=jax.ShapeDtypeStru...  78.4 us
    unnamed x1, local copies, waits for them, and re-layouts  1.67 us

profile of v2, /device:TPU:1, one launch (start us, length us, event | category | flops | bytes accessed | tf_op | source)
XLA Modules:
  0.0 80.8 jit_solution(4782447774854866516)
XLA Ops:
  0.7 78.4 %shard_map.55 = f32[512,128]{1,0:T(8,128)} custom-call(s32[1]{0:T(128)S(6)} %copy.7.colour_ref, s32[1,6]{1,0:T(1,128)} %tc_ref.1, f32[512,128]{1,0:T(8,128)} %res_hbm.1, f32[512,512]{1,0:T(8,128)} %inv_hbm.1, f32[6,512,512]{2,1,0:T(8,128)} %bitcast.1), custom_call_target="tpu_custom_call" | custom-call | tf_op jit(solution)/shard_map/pallas_call | solution.py:303
  79.1 1.7 %copy.8 = f32[512,128]{1,0:T(8,128)} copy(f32[512,128]{1,0:T(8,128)} %shard_map.55) | data formatting | bytes 524288

commit v3 on v2

--- a/solution.py
+++ b/solution.py
@@ -302,7 +302,7 @@
     hbm = pl.BlockSpec(memory_space=pl.ANY)
     return pl.pallas_call(
         functools.partial(kernel, n),
-        out_shape=jax.ShapeDtypeStruct((BLOCK, COLS), F32),
+        out_shape=pltpu.VMEM((BLOCK, COLS), F32),
         in_specs=[smem, smem, hbm, hbm, hbm],
         out_specs=pl.BlockSpec(memory_space=pltpu.VMEM),
         scratch_shapes=[

time: 80.9 us -> 79.2 us (0.979)
  local copies, waits for them, and re-layouts: 1.67 us -> 0.71 us
    unnamed x1, local copies, waits for them, and re-layouts: 1.67 us -> 0.71 us
where the time goes in v3:
time: 79.2 us; the launch traced here: 79.1 us
  Pallas kernels  77.7 us (98%)
    pallas_call x1, Pallas kernels, per_device(): pl.pallas_call(functools.partial(kernel, n), out_shape=pltpu.VMEM((BLOCK,...  77.7 us

profile of v3, /device:TPU:1, one launch (start us, length us, event | category | flops | bytes accessed | tf_op | source)
XLA Modules:
  0.0 79.1 jit_solution(8543523535888378008)
XLA Ops:
  0.7 77.7 %shard_map.55 = f32[512,128]{1,0:T(8,128)S(1)} custom-call(s32[1]{0:T(128)S(6)} %copy.8.colour_ref, s32[1,6]{1,0:T(1,128)} %tc_ref.1, f32[512,128]{1,0:T(8,128)} %res_hbm.1, f32[512,512]{1,0:T(8,128)} %inv_hbm.1, f32[6,512,512]{2,1,0:T(8,128)} %bitcast.1), custom_call_target="tpu_custom_call" | custom-call | tf_op jit(solution)/shard_map/pallas_call | solution.py:303
  78.4 0.7 copy.7
